TPU v7x, 512 devices: a whole 4x4x16 slice. The times are simulated.
512 devices in a mesh: factor: 16 (over x_hi, y, core), load: 32 (over z, x_lo).
Axes of the slice: x: 4 (x_hi: 2, x_lo: 2; x = x_hi * 2 + x_lo), y: 4, z: 16, core: 2. Of those that a mesh axis runs over, the one named last changes fastest.
Arguments:
- b_panel: bfloat16 [2048, 8192], P('factor', 'load'), may hold values from -6 to 6
- b_update: bfloat16 [8192, 8192], P('factor', 'load'), may hold values from -6 to 6
- panel_inverse: bfloat16 [2048, 2048], P('factor'), as said below
- update_factor: bfloat16 [8192, 2048], P('factor'), may hold values from -0.125 to 0.125
- update_solution: bfloat16 [8192, 8192], P(('factor', 'load')), may hold values from -3 to 3
- axle_weights: bfloat16 [3072, 8192], P('load'), may hold values from -0.0625 to 0.0625
Outputs:
- update_rhs: bfloat16 [8192, 8192], P('factor', 'load')
- panel_solution: bfloat16 [2048, 8192], P('factor', 'load')
- config_response: float32 [3072, 2048], P('load', 'factor')
Inputs may be any that keep to these rules, and one draw needn't show every extreme that they name: panel_inverse is zero above the diagonal and its diagonal lies between 1 and 2.
All inputs are finite; a program needn't handle non-finite values.
Results may differ from a plain program's by a relative error of at most 0.0052.
Values may be sent and summed in bfloat16 or wider, within the bound.
A program may use at most 64 MiB of HBM per device.

v0:
```python
import jax
import jax.numpy as jnp
from jax import lax
from jax.sharding import PartitionSpec as P


def local(b_panel, b_update, panel_inverse, update_factor, update_solution, axle_weights):
    block = panel_inverse
    forward = jnp.dot(
        block,
        lax.all_gather(b_panel, "factor", axis=0, tiled=True),
        preferred_element_type=jnp.float32,
    ).astype(jnp.bfloat16)
    block = update_factor
    lowered = jnp.dot(
        block,
        lax.all_gather(forward, "factor", axis=0, tiled=True),
        preferred_element_type=jnp.float32,
    )
    update_rhs = (b_update.astype(jnp.float32) - lowered).astype(jnp.bfloat16)
    regrouped = lax.all_to_all(update_solution, "load", split_axis=1, concat_axis=0, tiled=True)
    factor_cols = lax.all_to_all(update_factor, "factor", split_axis=1, concat_axis=0, tiled=True)
    block = factor_cols
    coupled = lax.dot_general(
        block,
        lax.all_gather(regrouped, "factor", axis=0, tiled=True),
        (((0,), (0,)), ((), ())),
        preferred_element_type=jnp.float32,
    )
    reduced = (forward.astype(jnp.float32) - coupled).astype(jnp.bfloat16)
    block = panel_inverse
    panel_solution = lax.psum_scatter(
        lax.dot_general(
            block, reduced, (((0,), (0,)), ((), ())), preferred_element_type=jnp.float32
        ),
        "factor",
        scatter_dimension=0,
        tiled=True,
    ).astype(jnp.bfloat16)
    block = axle_weights
    config_response = lax.dot_general(
        block,
        lax.all_gather(panel_solution, "load", axis=1, tiled=True),
        (((1,), (1,)), ((), ())),
        preferred_element_type=jnp.float32,
    )
    return (update_rhs, panel_solution, config_response)


def solution(mesh):
    in_specs = (
        P("factor", "load"),
        P("factor", "load"),
        P("factor", None),
        P("factor", None),
        P(("factor", "load"), None),
        P("load", None),
    )
    out_specs = (P("factor", "load"), P("factor", "load"), P("load", "factor"))
    return jax.shard_map(local, mesh=mesh, in_specs=in_specs, out_specs=out_specs, check_vma=False)
```

profile of v0, /device:TPU:8, one launch (start us, length us, event | category | flops | bytes accessed | tf_op | source)
XLA Modules:
  0.0 457.9 jit_solution(6282745598450169393)
XLA Ops:
  7.2 0.0 copy-start
  7.2 0.0 all-gather.5.cloned.1.call-start
  7.2 0.7 all-gather.5.cloned.1.call-update
  7.9 0.0 all-gather.9.cloned.1.call-start
  8.0 1.0 copy.29
  8.9 38.2 %all_to_all.38 = bf16[16,32,256]{2,0,1:T(8,128)(2,1)} all-to-all(bf16[16,32,256]{2,0,1:T(8,128)(2,1)S(1)} %bitcast.33), channel_id=1, replica_groups=mesh['factor'=16,'load'=32] {'load'}, dimensions={1} | all-to-all | bytes 524288 | tf_op jit(solution)/shard_map/all_to_all | solution.py:21
  47.1 0.0 all-gather.9.cloned.1.call-update
  47.2 0.0 reduce-scatter.2.cloned.1.call-start
  47.2 3.9 copy.22
  51.1 35.7 %all_to_all.39 = bf16[512,16,128]{0,2,1:T(8,128)(2,1)} all-to-all(bf16[512,16,128]{0,2,1:T(8,128)(2,1)} %bitcast.31), channel_id=1, replica_groups=mesh['factor'=16,'load'=32] {'factor'}, dimensions={1} | all-to-all | bytes 4194304 | tf_op jit(solution)/shard_map/all_to_all | solution.py:22
  86.8 0.0 copy-start.1
  86.8 4.0 copy.23
  90.8 0.0 all-gather.5.cloned.1.call-done
  90.8 0.0 copy-done.1
  90.8 1.5 convolution_convert_fusion
  92.3 0.0 copy-start.2
  92.4 58.4 %all-gather.9.cloned.1.call-done = bf16[8192,256]{1,0:T(8,128)(2,1)} async-done(((bf16[512,256]{1,0:T(8,128)(2,1)}), bf16[8192,256]{1,0:T(8,128)(2,1)}) %all-gather.9.cloned.1.call-update) | async-done | bytes 4194320 | tf_op jit(solution)/shard_map/all_gather | solution.py:26
  150.8 5.9 %convolution_bitcast_fusion = f32[2048,256]{0,1:T(8,128)} fusion(bf16[128,2048]{1,0:T(8,128)(2,1)S(1)} %copy-done.1, bf16[8192,128]{1,0:T(8,128)(2,1)} %bitcast.29, bf16[8192,256]{1,0:T(8,128)(2,1)} %all-gather.9.cloned.1.call-done, bf16[128,256]{1,0:T(8,128)(2,1)S(1)} %convolution_convert_fusion), kind=kOutput, calls=%fused_computation | convolution fusion | flops 671186944 | bytes 8978432 | tf_op jit(solution)/shard_map/dot_general | solution.py:33
  156.6 0.0 copy-done.2
  156.6 0.0 copy-start.4
  156.6 0.0 reduce-scatter.2.cloned.1.call-update
  156.7 0.0 all-gather.7.cloned.1.call-start
  156.7 0.5 all-gather.7.cloned.1.call-update
  157.2 0.0 all-gather.11.cloned.1.call-start
  157.3 92.5 %reduce-scatter.2.cloned.1.call-done = f32[128,256]{0,1:T(8,128)} async-done(((f32[2048,256]{0,1:T(8,128)}), f32[128,256]{0,1:T(8,128)}) %reduce-scatter.2.cloned.1.call-update) | async-done | bytes 131088 | tf_op jit(solution)/shard_map/reduce_scatter | solution.py:32
  249.8 1.5 convert_element_type.23
  251.3 0.0 all-gather.11.cloned.1.call-update
  251.3 0.0 copy-done.4
  251.3 0.1 copy.21
  251.5 0.0 copy-start.3
  251.5 61.9 %all-gather.7.cloned.1.call-done = bf16[2048,256]{1,0:T(8,128)(2,1)} async-done(((bf16[128,256]{1,0:T(8,128)(2,1)}), bf16[2048,256]{1,0:T(8,128)(2,1)}) %all-gather.7.cloned.1.call-update) | async-done | bytes 1048592 | tf_op jit(solution)/shard_map/all_gather | solution.py:17
  313.4 2.7 fusion.1
  316.0 0.8 copy.25
  316.9 0.0 copy-done.3
  316.9 0.7 copy.26
  317.6 131.0 %all-gather.11.cloned.1.call-done = bf16[128,8192]{0,1:T(8,128)(2,1)} async-done(((bf16[128,256]{0,1:T(8,128)(2,1)}), bf16[128,8192]{0,1:T(8,128)(2,1)}) %all-gather.11.cloned.1.call-update) | async-done | bytes 2097168 | tf_op jit(solution)/shard_map/all_gather | solution.py:43
  448.6 0.0 copy-done
  448.6 2.8 convolution_bitcast_fusion.2
Async XLA Ops:
  7.2 441.5 %copy-start = (bf16[96,8192]{1,0:T(8,128)(2,1)S(1)}, bf16[96,8192]{1,0:T(8,128)(2,1)}, u32[]{:S(2)}) copy-start(bf16[96,8192]{1,0:T(8,128)(2,1)} %param.11) | copy-start | bytes 4718596
  7.2 83.6 %all-gather.5.cloned.1.call-start = ((), (), s32[]{:S(2)}) async-start(), calls=%async_computation.3 | async-start | bytes 1114112 | tf_op jit(solution)/shard_map/all_gather | solution.py:11
  7.9 142.8 %all-gather.9.cloned.1.call-start = ((), (), s32[]{:S(2)}) async-start(), calls=%async_computation.5 | async-start | bytes 4456448 | tf_op jit(solution)/shard_map/all_gather | solution.py:26
  47.2 202.6 %reduce-scatter.2.cloned.1.call-start = ((), (), s32[]{:S(2)}) async-start(), calls=%async_computation.6 | async-start | bytes 2228224 | tf_op jit(solution)/shard_map/reduce_scatter | solution.py:32
  86.8 4.0 copy-start.1
  92.3 64.3 %copy-start.2 = (bf16[128,256]{1,0:T(8,128)(2,1)}, bf16[128,256]{1,0:T(8,128)(2,1)S(1)}, u32[]{:S(2)}) copy-start(bf16[128,256]{1,0:T(8,128)(2,1)S(1)} %convolution_convert_fusion) | copy-start | bytes 196612
  156.6 94.7 %copy-start.4 = (bf16[512,256]{1,0:T(8,128)(2,1)S(1)}, bf16[512,256]{1,0:T(8,128)(2,1)}, u32[]{:S(2)}) copy-start(bf16[512,256]{1,0:T(8,128)(2,1)} %param.7) | copy-start | bytes 786436
  156.7 156.7 %all-gather.7.cloned.1.call-start = ((), (), s32[]{:S(2)}) async-start(), calls=%async_computation.4 | async-start | bytes 1114112 | tf_op jit(solution)/shard_map/all_gather | solution.py:17
  157.2 291.4 %all-gather.11.cloned.1.call-start = ((), (), s32[]{:S(2)}) async-start(), calls=%async_computation.7 | async-start | bytes 2162688 | tf_op jit(solution)/shard_map/all_gather | solution.py:43
  251.5 65.4 %copy-start.3 = (bf16[128,256]{0,1:T(8,128)(2,1)S(1)}, bf16[128,256]{0,1:T(8,128)(2,1)}, u32[]{:S(2)}) copy-start(bf16[128,256]{0,1:T(8,128)(2,1)} %convert_element_type.23) | copy-start | bytes 196612
Sparse Core Ops, SparseCore 0:
  11.4 67.5 all-gather.4
  82.3 68.3 all-gather.8
  156.8 92.9 reduce-scatter.1
  254.1 59.2 all-gather.6
  315.5 133.0 all-gather.10
where the time goes:
time: 458 us
  waiting for transfers between devices  345 us (75%)
  blocking collectives  73.9 us (16%)
  between operations  13.8 us (3%)
  matrix products  12.9 us (3%)
  local copies, waits for them, and re-layouts  10.7 us (2%)
    all_gather x1, waiting for transfers between devices, local(): lax.all_gather(panel_solution, 'load', axis=1, tiled=True)  131 us
    reduce_scatter x1, waiting for transfers between devices, local(): lax.psum_scatter(lax.dot_general(block, reduced, (((0,), (0,)), ((), ()))...  92.5 us
    all_gather x1, waiting for transfers between devices, local(): lax.all_gather(forward, 'factor', axis=0, tiled=True)  61.9 us
    all_gather x1, waiting for transfers between devices, local(): lax.all_gather(regrouped, 'factor', axis=0, tiled=True)  58.4 us
    all_to_all x1, blocking collectives, local(): lax.all_to_all(update_solution, 'load', split_axis=1, concat_axis=0, tile...  38.2 us
    all_to_all x1, blocking collectives, local(): lax.all_to_all(update_factor, 'factor', split_axis=1, concat_axis=0, tile...  35.7 us
  transfers between devices with their start and end apart: 5, of which 4 were waited for; matrix products, arithmetic and copies ran while one was open for 4% of the time, Pallas kernels for 0%

commit v1 on v0

--- a/solution.py
+++ b/solution.py
@@ -1,7 +1,17 @@
+import functools
 import jax
 import jax.numpy as jnp
 from jax import lax
 from jax.sharding import PartitionSpec as P
+from jax.lax import all_to_all, axis_size
+
+
+def remake_routes_all(state, dim_k):
+    p_next = all_to_all(jnp.stack(axis_size("load") * [state], axis=0), "load", 0, 0)
+    return jnp.concatenate(p_next, axis=dim_k)
+
+
+counts_lead = functools.partial(remake_routes_all, dim_k=1)
 
 
 def local(b_panel, b_update, panel_inverse, update_factor, update_solution, axle_weights):
@@ -40,7 +50,7 @@
     block = axle_weights
     config_response = lax.dot_general(
         block,
-        lax.all_gather(panel_solution, "load", axis=1, tiled=True),
+        counts_lead(panel_solution),
         (((1,), (1,)), ((), ())),
         preferred_element_type=jnp.float32,
     )

time: 458 us -> 374 us (0.82)
  the two profiles are of different devices: /device:TPU:8 before, /device:TPU:2 now
where the time goes in v1:
time: 374 us; the launch traced here: 373 us
  waiting for transfers between devices  242 us (65%)
  blocking collectives  76.4 us (20%)
  starting transfers between devices  14.1 us (4%)
  between operations  13.8 us (4%)
  matrix products  12.9 us (3%)
  local copies, waits for them, and re-layouts  12.4 us (3%)
    reduce_scatter x1, waiting for transfers between devices, local(): lax.psum_scatter(lax.dot_general(block, reduced, (((0,), (0,)), ((), ()))...  92.4 us
    all_gather x1, waiting for transfers between devices, local(): lax.all_gather(forward, 'factor', axis=0, tiled=True)  62.6 us
    all_gather x1, waiting for transfers between devices, local(): lax.all_gather(regrouped, 'factor', axis=0, tiled=True)  56.2 us
    all_to_all x1, blocking collectives, local(): lax.all_to_all(update_factor, 'factor', split_axis=1, concat_axis=0, tile...  38.3 us
    all_to_all x1, blocking collectives, local(): lax.all_to_all(update_solution, 'load', split_axis=1, concat_axis=0, tile...  38.2 us
    all_to_all x1, waiting for transfers between devices, remake_routes_all(): all_to_all(jnp.stack(axis_size('load') * [state], axis=0), 'load', 0, 0)  30.1 us
    all_to_all x1, starting transfers between devices, remake_routes_all(): all_to_all(jnp.stack(axis_size('load') * [state], axis=0), 'load', 0, 0)  14 us
  transfers between devices with their start and end apart: 5, of which 4 were waited for; matrix products, arithmetic and copies ran while one was open for 4% of the time, Pallas kernels for 0%

profile of v1, /device:TPU:2, one launch (start us, length us, event | category | flops | bytes accessed | tf_op | source)
XLA Modules:
  0.0 373.1 jit_solution(2086332847864899456)
XLA Ops:
  7.2 0.0 copy-start
  7.2 0.0 all-gather.4.cloned.1.call-start
  7.2 0.7 all-gather.4.cloned.1.call-update
  7.9 0.0 all-gather.8.cloned.1.call-start
  8.0 1.0 copy.30
  8.9 38.2 %all_to_all.43 = bf16[16,32,256]{2,0,1:T(8,128)(2,1)} all-to-all(bf16[16,32,256]{2,0,1:T(8,128)(2,1)S(1)} %bitcast.36), channel_id=1, replica_groups=mesh['factor'=16,'load'=32] {'load'}, dimensions={1} | all-to-all | bytes 524288 | tf_op jit(solution)/shard_map/all_to_all | solution.py:31
  47.1 0.0 all-gather.8.cloned.1.call-update
  47.1 0.0 reduce-scatter.2.cloned.1.call-start
  47.2 3.9 %copy.23 = bf16[512,2048]{0,1:T(8,128)(2,1)} copy(bf16[512,2048]{1,0:T(8,128)(2,1)} %param.9) | data formatting | bytes 4194304 | tf_op args[3]
  51.1 38.3 %all_to_all.44 = bf16[512,16,128]{0,2,1:T(8,128)(2,1)} all-to-all(bf16[512,16,128]{0,2,1:T(8,128)(2,1)} %bitcast.34), channel_id=1, replica_groups=mesh['factor'=16,'load'=32] {'factor'}, dimensions={1} | all-to-all | bytes 4194304 | tf_op jit(solution)/shard_map/all_to_all | solution.py:32
  89.4 0.0 copy-start.1
  89.4 4.0 %copy.24 = bf16[16,512,128]{2,1,0:T(8,128)(2,1)} copy(bf16[16,512,128]{1,2,0:T(8,128)(2,1)} %bitcast.33) | data formatting | bytes 4194304 | tf_op jit(solution)/shard_map/all_to_all | solution.py:32
  93.4 0.0 all-gather.4.cloned.1.call-done
  93.4 0.0 copy-done.1
  93.4 1.5 convolution_convert_fusion
  94.9 0.0 copy-start.2
  94.9 56.2 %all-gather.8.cloned.1.call-done = bf16[8192,256]{1,0:T(8,128)(2,1)} async-done(((bf16[512,256]{1,0:T(8,128)(2,1)}), bf16[8192,256]{1,0:T(8,128)(2,1)}) %all-gather.8.cloned.1.call-update) | async-done | bytes 4194320 | tf_op jit(solution)/shard_map/all_gather | solution.py:36
  151.1 5.9 %convolution_bitcast_fusion = f32[2048,256]{0,1:T(8,128)} fusion(bf16[128,2048]{1,0:T(8,128)(2,1)S(1)} %copy-done.1, bf16[8192,128]{1,0:T(8,128)(2,1)} %bitcast.32, bf16[8192,256]{1,0:T(8,128)(2,1)} %all-gather.8.cloned.1.call-done, bf16[128,256]{1,0:T(8,128)(2,1)S(1)} %convolution_convert_fusion), kind=kOutput, calls=%fused_computation | convolution fusion | flops 671186944 | bytes 8978432 | tf_op jit(solution)/shard_map/dot_general | solution.py:43
  157.0 0.0 copy-done.2
  157.0 0.0 reduce-scatter.2.cloned.1.call-update
  157.0 92.4 %reduce-scatter.2.cloned.1.call-done = f32[128,256]{0,1:T(8,128)} async-done(((f32[2048,256]{0,1:T(8,128)}), f32[128,256]{0,1:T(8,128)}) %reduce-scatter.2.cloned.1.call-update) | async-done | bytes 131088 | tf_op jit(solution)/shard_map/reduce_scatter | solution.py:42
  249.4 0.9 convert_element_type.23
  250.3 1.8 stack.2
  252.1 0.0 copy-start.3
  252.1 14.0 %all-to-all-start.2 = ((bf16[32,128,256]{1,2,0:T(8,128)(2,1)}), bf16[32,128,256]{1,2,0:T(8,128)(2,1)}, u32[]{:S(2)}, u32[]{:S(2)}) async-start(bf16[32,128,256]{1,2,0:T(8,128)(2,1)} %stack.2), calls=%async_computation.3 | async-start | bytes 4194304 | tf_op jit(solution)/shard_map/all_to_all | solution.py:10
  266.1 0.0 all-gather.6.cloned.1.call-start
  266.2 0.5 all-gather.6.cloned.1.call-update
  266.7 0.0 copy-done.3
  266.7 0.1 copy.22
  266.8 62.6 %all-gather.6.cloned.1.call-done = bf16[2048,256]{1,0:T(8,128)(2,1)} async-done(((bf16[128,256]{1,0:T(8,128)(2,1)}), bf16[2048,256]{1,0:T(8,128)(2,1)}) %all-gather.6.cloned.1.call-update) | async-done | bytes 1048592 | tf_op jit(solution)/shard_map/all_gather | solution.py:27
  329.4 2.7 fusion.1
  332.1 0.8 copy.26
  332.9 0.7 copy.27
  333.7 30.1 %all-to-all-done.2 = bf16[32,128,256]{1,2,0:T(8,128)(2,1)} async-done(((bf16[32,128,256]{1,2,0:T(8,128)(2,1)}), bf16[32,128,256]{1,2,0:T(8,128)(2,1)}, u32[]{:S(2)}, u32[]{:S(2)}) %all-to-all-start.2) | async-done | bytes 2097184 | tf_op jit(solution)/shard_map/all_to_all | solution.py:10
  363.7 0.0 copy-done
  363.7 2.8 convolution_bitcast_fusion.2
Async XLA Ops:
  7.2 356.6 %copy-start = (bf16[96,8192]{1,0:T(8,128)(2,1)S(1)}, bf16[96,8192]{1,0:T(8,128)(2,1)}, u32[]{:S(2)}) copy-start(bf16[96,8192]{1,0:T(8,128)(2,1)} %param.11) | copy-start | bytes 4718596
  7.2 86.2 %all-gather.4.cloned.1.call-start = ((), (), s32[]{:S(2)}) async-start(), calls=%async_computation.4 | async-start | bytes 1114112 | tf_op jit(solution)/shard_map/all_gather | solution.py:21
  7.9 143.2 %all-gather.8.cloned.1.call-start = ((), (), s32[]{:S(2)}) async-start(), calls=%async_computation.6 | async-start | bytes 4456448 | tf_op jit(solution)/shard_map/all_gather | solution.py:36
  47.1 202.3 %reduce-scatter.2.cloned.1.call-start = ((), (), s32[]{:S(2)}) async-start(), calls=%async_computation.7 | async-start | bytes 2228224 | tf_op jit(solution)/shard_map/reduce_scatter | solution.py:42
  89.4 4.0 %copy-start.1 = (bf16[128,2048]{1,0:T(8,128)(2,1)S(1)}, bf16[128,2048]{1,0:T(8,128)(2,1)}, u32[]{:S(2)}) copy-start(bf16[128,2048]{1,0:T(8,128)(2,1)} %param.8) | copy-start | bytes 1572868
  94.9 62.1 %copy-start.2 = (bf16[128,256]{1,0:T(8,128)(2,1)}, bf16[128,256]{1,0:T(8,128)(2,1)S(1)}, u32[]{:S(2)}) copy-start(bf16[128,256]{1,0:T(8,128)(2,1)S(1)} %convolution_convert_fusion) | copy-start | bytes 196612
  252.1 14.6 %copy-start.3 = (bf16[512,256]{1,0:T(8,128)(2,1)S(1)}, bf16[512,256]{1,0:T(8,128)(2,1)}, u32[]{:S(2)}) copy-start(bf16[512,256]{1,0:T(8,128)(2,1)} %param.7) | copy-start | bytes 786436
  252.1 111.6 %all-to-all-start.2 = ((bf16[32,128,256]{1,2,0:T(8,128)(2,1)}), bf16[32,128,256]{1,2,0:T(8,128)(2,1)}, u32[]{:S(2)}, u32[]{:S(2)}) async-start(bf16[32,128,256]{1,2,0:T(8,128)(2,1)} %stack.2), calls=%async_computation.3 | async-start | bytes 4194304 | tf_op jit(solution)/shard_map/all_to_all | solution.py:10
  266.1 63.3 %all-gather.6.cloned.1.call-start = ((), (), s32[]{:S(2)}) async-start(), calls=%async_computation.5 | async-start | bytes 1114112 | tf_op jit(solution)/shard_map/all_gather | solution.py:27
Sparse Core Ops, SparseCore 0:
  11.4 68.2 all-gather.3
  82.9 68.1 all-gather.7
  157.2 92.1 reduce-scatter.1
  271.1 58.2 all-gather.5
